TPU v7x, 32 devices: a whole 2x2x4 slice. The times are simulated.
32 devices in a mesh: prow: 8 (over y, x, core), pcol: 4 (over z).
Axes of the slice: x: 2, y: 2, z: 4, core: 2. Of those that a mesh axis runs over, the one named last changes fastest.
Arguments:
- cov_trail: float32 [1024, 1024], P('prow', 'pcol'), as said below
- factor_panel: bfloat16 [4, 1024, 128], P(None, 'prow'), may hold values from -0.25 to 0.25
- first_level: int32 [8], replicated, may hold values from 0 to 4
- block_slot: int32 [8], replicated, may hold values from 0 to 7, each once
- factor_window: bfloat16 [6, 128, 128], replicated, may hold values from -0.5 to 0.5
- diag_inverse: float32 [4, 128, 128], replicated, as said below
Outputs:
- panel_cov: float32 [4, 1024, 128], P(None, 'prow')
- window_cov: float32 [512, 512], replicated
Inputs may be any that keep to these rules, and one draw needn't show every extreme that they name: Trailing block j lies in the pattern of window supernode k exactly when first_level[j] <= k, so the patterns are nested. `block_slot`: a permutation; slot s is held by process row s // 1 and process column s // (8 / pcol size), slots in contiguous blocks. `cov_trail`: symmetric. `diag_inverse`: each block symmetric.
All inputs are finite; a program needn't handle non-finite values.
Results may differ from a plain program's by a relative error of at most 0.0003.
Values may be sent and summed in bfloat16 or wider, within the bound.
A program may use at most 64 MiB of HBM per device.

v0:
```python
import jax
import jax.numpy as jnp
from jax import lax
from jax.sharding import PartitionSpec as P


def pair_index(upper, lower, window_count):
    return lower * window_count - lower * (lower + 1) // 2 + upper - lower - 1


def later_block(window, upper, lower):
    if upper >= lower:
        return window[upper, lower]
    return window[lower, upper].T


def window_step(window, cross_sums, diag_term, later_nodes, window_factor, diag_block, supernode):
    highest = lax.Precision.HIGHEST
    for place, upper in enumerate(later_nodes):
        block_total = cross_sums[place]
        for second, other in enumerate(later_nodes):
            block_total = block_total + jnp.dot(
                later_block(window, upper, other),
                window_factor[second],
                precision=highest,
                preferred_element_type=jnp.float32,
            )
        window[upper, supernode] = -block_total
    diagonal = diag_block - diag_term
    for place, upper in enumerate(later_nodes):
        diagonal = diagonal - jnp.dot(
            window_factor[place].T,
            window[upper, supernode],
            precision=highest,
            preferred_element_type=jnp.float32,
        )
    window[supernode, supernode] = diagonal


def shards(cov_trail, factor_panel, first_level, block_slot, factor_window, diag_inverse):
    highest = lax.Precision.HIGHEST
    block_size = diag_inverse.shape[-1]
    window_count = diag_inverse.shape[0]
    rows_loc = cov_trail.shape[0]
    cols_loc = cov_trail.shape[1]
    block_count = first_level.shape[0]
    slot_ids = lax.iota(jnp.int32, block_count)
    level_slot = jnp.sum(
        jnp.where(block_slot[None, :] == slot_ids[:, None], first_level[None, :], 0), axis=1
    )
    local_blocks = rows_loc // block_size
    row_level = jnp.repeat(
        lax.dynamic_slice_in_dim(level_slot, lax.axis_index("prow") * local_blocks, local_blocks),
        block_size,
    )
    columns = {}
    window = {}
    for supernode in range(window_count - 1, -1, -1):
        keep_rows = (row_level <= supernode)[:, None]
        panel_row = jnp.where(keep_rows, factor_panel[supernode], jnp.zeros((), jnp.bfloat16))
        gathered = lax.all_gather(panel_row, "prow", axis=0, tiled=True)
        panel_col = lax.dynamic_slice_in_dim(
            gathered, lax.axis_index("pcol") * cols_loc, cols_loc, 0
        )
        panel_full = panel_row.astype(jnp.float32)
        partial_prod = jnp.dot(
            cov_trail,
            panel_col.astype(jnp.float32),
            precision=highest,
            preferred_element_type=jnp.float32,
        )
        later_nodes = list(range(supernode + 1, window_count))
        window_factor = [
            factor_window[pair_index(upper, supernode, window_count)].astype(jnp.float32)
            for upper in later_nodes
        ]
        summed = lax.psum(partial_prod, "pcol")
        accumulated = summed
        for place, upper in enumerate(later_nodes):
            accumulated = accumulated + jnp.dot(
                columns[upper],
                window_factor[place],
                precision=highest,
                preferred_element_type=jnp.float32,
            )
        new_column = jnp.where(keep_rows, -accumulated, jnp.float32(0.0))
        columns[supernode] = new_column
        term_list = []
        for upper in later_nodes:
            term_list.append(
                jnp.dot(
                    columns[upper].T,
                    panel_full,
                    precision=highest,
                    preferred_element_type=jnp.float32,
                )
            )
        term_list.append(
            jnp.dot(panel_full.T, new_column, precision=highest, preferred_element_type=jnp.float32)
        )
        cross_sums = lax.psum(jnp.stack(term_list), "prow")
        diag_term = cross_sums[len(later_nodes)]
        window_step(
            window,
            cross_sums,
            diag_term,
            later_nodes,
            window_factor,
            diag_inverse[supernode],
            supernode,
        )
    panel_cov = jnp.stack([columns[supernode] for supernode in range(window_count)])
    block_rows = [
        jnp.concatenate(
            [later_block(window, upper, other) for other in range(window_count)], axis=1
        )
        for upper in range(window_count)
    ]
    window_cov = jnp.concatenate(block_rows, axis=0)
    return (panel_cov, window_cov)


def solution(mesh):
    return jax.shard_map(
        shards,
        mesh=mesh,
        in_specs=(P("prow", "pcol"), P(None, "prow", None), P(), P(), P(), P()),
        out_specs=(P(None, "prow", None), P()),
        check_vma=False,
    )
```

profile of v0, /device:TPU:1, one launch (start us, length us, event | category | flops | bytes accessed | tf_op | source)
XLA Modules:
  0.0 167.8 jit_solution(11450177156620109265)
XLA Ops:
  7.3 0.7 copy-done.9
  8.0 0.6 dynamic_slice.15
  11.2 0.8 slice_select_fusion.3
  12.1 10.7 %all-gather.3 = bf16[1,1024,128]{2,1,0:T(8,128)(2,1)S(1)} all-gather(bf16[1,128,128]{2,1,0:T(8,128)(2,1)S(1)} %get-tuple-element.20), channel_id=5, replica_groups=mesh['prow'=8,'pcol'=4] {'prow'}, dimensions={1}, use_global_device_ids=true | all-gather | bytes 294912 | tf_op jit(solution)/shard_map/all_gather | solution.py:61
  22.7 9.3 %all-gather.2 = bf16[1,1024,128]{2,1,0:T(8,128)(2,1)S(1)} all-gather(bf16[1,128,128]{2,1,0:T(8,128)(2,1)S(1)} %get-tuple-element.21), channel_id=4, replica_groups=mesh['prow'=8,'pcol'=4] {'prow'}, dimensions={1}, use_global_device_ids=true | all-gather | bytes 294912 | tf_op jit(solution)/shard_map/all_gather | solution.py:61
  32.0 0.9 convolution_bitcast_fusion.16
  32.9 0.9 convolution_bitcast_fusion.17
  33.8 8.3 %all-gather.1 = bf16[1,1024,128]{2,1,0:T(8,128)(2,1)S(1)} all-gather(bf16[1,128,128]{2,1,0:T(8,128)(2,1)S(1)} %get-tuple-element.19), channel_id=3, replica_groups=mesh['prow'=8,'pcol'=4] {'prow'}, dimensions={1}, use_global_device_ids=true | all-gather | bytes 294912 | tf_op jit(solution)/shard_map/all_gather | solution.py:61
  42.1 0.9 convolution_bitcast_fusion.18
  43.0 9.3 %all-gather = bf16[1,1024,128]{2,1,0:T(8,128)(2,1)S(1)} all-gather(bf16[1,128,128]{2,1,0:T(8,128)(2,1)S(1)} %get-tuple-element.18), channel_id=2, replica_groups=mesh['prow'=8,'pcol'=4] {'prow'}, dimensions={1}, use_global_device_ids=true | all-gather | bytes 294912 | tf_op jit(solution)/shard_map/all_gather | solution.py:61
  52.3 0.9 convolution_bitcast_fusion.19
  53.2 34.3 %all-reduce.7.cloned.1.call-done = (f32[128,128]{0,1:T(8,128)}, f32[128,128]{0,1:T(8,128)}, f32[128,128]{0,1:T(8,128)}, f32[128,128]{0,1:T(8,128)}) async-done(((f32[128,128]{0,1:T(8,128)}, f32[128,128]{0,1:T(8,128)}, f32[128,128]{0,1:T(8,128)}, f32[128,128]{0,1:T(8,128)}), (f32[128,128]{0,1:T(8,128)}, f32[128,128]{0,1:T(8,128)}, f32[128,128]{0,1:T(8,128)}, ...) | async-done | bytes 262160 | tf_op jit(solution)/shard_map/psum | solution.py:77
  87.5 1.1 fusion.17
  88.9 0.6 copy-done.1
  91.3 1.7 convolution_bitcast_fusion.6
  93.5 0.2 fusion.13
  94.0 0.7 pad_maximum_fusion.4
  94.6 0.7 pad_maximum_fusion.3
  95.3 0.7 pad_maximum_fusion.1
  96.1 0.8 copy.67
  97.0 55.4 %all-reduce.5.cloned.1.call-done = (f32[1,128,128]{2,1,0:T(8,128)}, f32[2,128,128]{1,2,0:T(8,128)}, f32[3,128,128]{2,1,0:T(8,128)}, f32[4,128,128]{2,1,0:T(8,128)}) async-done(((f32[1,128,128]{2,1,0:T(8,128)}, f32[2,128,128]{1,2,0:T(8,128)}, f32[3,128,128]{2,1,0:T(8,128)}, f32[4,128,128]{2,1,0:T(8,128)}), (f32[1,128,128]{2,1,0:T(8,128)}, f32[2,128,128]{1,2,0:T(8,128)}, f32[3,128,128]{2,1,0:T(8,128)}, ...) | async-done | bytes 655376 | tf_op jit(solution)/shard_map/psum | solution.py:101
  152.4 1.0 fusion.103
  153.7 0.6 copy-done.5
  154.3 0.2 convolution_add_fusion.10
  154.9 0.2 convolution_add_fusion.12
  155.5 0.4 copy-done.3
  156.1 0.2 convolution_add_fusion.1
  157.5 0.2 convolution_add_fusion.8
  158.0 0.2 fusion.5
  158.9 0.2 fusion.3
  159.3 0.2 fusion.2
  159.9 1.1 maximum_maximum_fusion
  (61 shorter events, 6.7 us)
Async XLA Ops:
  7.2 24.8 %copy-start = (f32[128,256]{1,0:T(8,128)S(1)}, f32[128,256]{1,0:T(8,128)}, u32[]{:S(2)}) copy-start(f32[128,256]{1,0:T(8,128)} %param.6) | copy-start | bytes 393220
  7.2 80.3 %all-reduce.7.cloned.1.call-start = ((), (), s32[]{:S(2)}) async-start(), calls=%async_computation.1 | async-start | bytes 524288 | tf_op jit(solution)/shard_map/psum | solution.py:77
  7.2 0.7 copy-start.9
  7.2 0.7 copy-start.10
  53.2 34.4 %copy-start.2 = (bf16[6,128,128]{2,1,0:T(8,128)(2,1)S(1)}, bf16[6,128,128]{2,1,0:T(8,128)(2,1)}, u32[]{:S(2)}) copy-start(bf16[6,128,128]{2,1,0:T(8,128)(2,1)} %param.10) | copy-start | bytes 589828
  53.2 99.2 %all-reduce.5.cloned.1.call-start = ((), (), s32[]{:S(2)}) async-start(), calls=%async_computation | async-start | bytes 1310720 | tf_op jit(solution)/shard_map/psum | solution.py:101
  87.5 1.2 copy-start.8
  88.7 0.8 copy-start.1
  91.3 1.7 copy-start.7
  96.1 56.3 %copy-start.4 = (f32[4,128,128]{2,1,0:T(8,128)S(1)}, f32[4,128,128]{2,1,0:T(8,128)}, u32[]{:S(2)}) copy-start(f32[4,128,128]{2,1,0:T(8,128)} %param.11) | copy-start | bytes 786436
  152.4 1.0 copy-start.6
  153.4 0.9 copy-start.5
  154.9 1.0 copy-start.3
Sparse Core Ops, SparseCore 0:
  53.3 34.1 all-reduce.6
  96.2 56.1 all-reduce.4
where the time goes:
time: 170 us; the launch traced here: 168 us
  waiting for transfers between devices  89.7 us (53%)
  blocking collectives  37.5 us (22%)
  between operations  17.1 us (10%)
  matrix products  13.7 us (8%)
  other arithmetic  5.08 us (3%)
  local copies, waits for them, and re-layouts  4.56 us (3%)
    psum x1, waiting for transfers between devices, shards(): cross_sums = lax.psum(jnp.stack(term_list), 'prow')  55.4 us
    all_gather x4, blocking collectives, shards(): gathered = lax.all_gather(panel_row, 'prow', axis=0, tiled=True)  37.5 us
    psum x1, waiting for transfers between devices, shards(): summed = lax.psum(partial_prod, 'pcol')  34.3 us
    dot_general x4, matrix products, shards(): jnp.dot(cov_trail, panel_col.astype(jnp.float32), precision=highest, pref...  3.56 us
    unnamed x26, local copies, waits for them, and re-layouts  3.41 us
  transfers between devices with their start and end apart: 2, of which 2 were waited for; matrix products, arithmetic and copies ran while one was open for 1% of the time, Pallas kernels for 0%

commit v1 on v0

v1 whole, which is shorter than its diff:
```python
import functools

import jax
import jax.numpy as jnp
from jax import lax
from jax.experimental import pallas as pl
from jax.experimental.pallas import tpu as pltpu
from jax.sharding import PartitionSpec as P

MESH = pl.DeviceIdType.MESH
F32 = jnp.float32
BF16 = jnp.bfloat16


def pair_index(upper, lower, window_count):
    return lower * window_count - lower * (lower + 1) // 2 + upper - lower - 1


def split(value):
    high = value.astype(BF16)
    return high, (value - high.astype(F32)).astype(BF16)


def dot(left, right):
    return jnp.dot(left, right, preferred_element_type=F32)


def kernel(
    sizes,
    first_ref,
    slot_ref,
    cov_ref,
    panel_ref,
    factor_ref,
    diag_ref,
    column_ref,
    window_ref,
    panels,
    masked,
    panel_t,
    factor_t,
    product,
    product_in,
    sums,
    inner,
    inner_in,
    pieces,
    x_parts,
    w_parts,
    panel_send,
    panel_fwd,
    panel_recv,
    product_send,
    product_recv,
    sums_send,
    sums_recv,
    inner_send,
    inner_recv,
    piece_send,
    piece_recv,
    row_send,
    row_fwd,
    row_recv,
):
    n_row, n_col, window_count, block = sizes
    local_blocks = cov_ref.shape[1] // block
    n_chip = n_row // 2
    width = window_count * block
    block_count = first_ref.shape[0]
    row_blocks = cov_ref.shape[0] // block
    chunk = product.shape[2]
    piece_rows = width // n_row
    me = lax.axis_index("prow")
    col = lax.axis_index("pcol")
    core = lax.rem(me, 2)
    chip = me // 2
    partner = chip * 2 + 1 - core

    def remote(src, dst, send, recv, row, column):
        return pltpu.make_async_remote_copy(
            src_ref=src,
            dst_ref=dst,
            send_sem=send,
            recv_sem=recv,
            device_id=(row, column),
            device_id_type=MESH,
        )

    def level_of(slot):
        level = jnp.int32(0)
        for index in range(block_count):
            level = level + jnp.where(slot_ref[index] == slot, first_ref[index], 0)
        return level

    barrier = pltpu.get_barrier_semaphore()
    for step in range(1, n_row):
        pl.semaphore_signal(
            barrier, inc=1, device_id=(lax.rem(me + step, n_row), col), device_id_type=MESH
        )
    for step in range(1, n_col):
        pl.semaphore_signal(
            barrier, inc=1, device_id=(me, lax.rem(col + step, n_col)), device_id_type=MESH
        )
    pl.semaphore_wait(barrier, n_row + n_col - 2)

    for turn in range(local_blocks // 2):
        mine = 2 * turn + core
        owner = col * local_blocks + mine

        @pl.when(me == owner)
        def _():
            for step in range(1, n_chip):
                target = lax.rem(chip + step, n_chip) * 2 + core
                remote(
                    panel_ref, panels.at[mine], panel_send.at[turn, step], panel_recv.at[mine], target, col
                ).start()
            remote(
                panel_ref, panels.at[mine], panel_fwd.at[turn], panel_recv.at[mine], partner, col
            ).start()
            panels[mine] = panel_ref[...]

    own_level = level_of(me)
    for k in range(window_count):
        own = jnp.where(own_level <= k, panel_ref[k].astype(F32), 0.0)
        panel_t[pl.ds(k * block, block), :] = own.T.astype(BF16)
    for index in range(factor_ref.shape[0]):
        factor_t[index] = factor_ref[index].astype(F32).T.astype(BF16)
    cov_high, cov_low = split(cov_ref[...])
    cov_parts = jnp.concatenate([cov_high, cov_low], axis=0)

    for turn in range(local_blocks // 2):
        mine = 2 * turn + core
        owner = col * local_blocks + mine

        @pl.when(me != owner)
        def _():
            forward = remote(
                panels.at[mine], panels.at[mine], panel_fwd.at[turn], panel_recv.at[mine], partner, col
            )
            forward.wait_recv()
            forward.start()

    for turn in range(local_blocks // 2):
        other = 2 * turn + 1 - core
        remote(
            panels.at[other], panels.at[other], panel_fwd.at[turn], panel_recv.at[other], partner, col
        ).wait_recv()

    for index in range(local_blocks):
        level = level_of(col * local_blocks + index)
        for k in range(window_count):
            masked[pl.ds(index * block, block), pl.ds(k * block, block)] = jnp.where(
                level <= k, panels[index, k].astype(F32), 0.0
            ).astype(BF16)

    rows = cov_ref.shape[0]
    both = dot(cov_parts, masked[...])
    partial = both[:rows] + both[rows:]
    for index in range(n_col):
        product[index] = partial[:, index * chunk : (index + 1) * chunk]
    for step in range(1, n_col):
        target = lax.rem(col + step, n_col)
        remote(
            product.at[target], product_in.at[col], product_send.at[step], product_recv.at[col], me, target
        ).start()
    total = product[col]
    for step in range(1, n_col):
        source = lax.rem(col + step, n_col)
        remote(
            product.at[source], product_in.at[source], product_send.at[step], product_recv.at[source], me, source
        ).wait_recv()
        total = total + product_in[source]
    sums[col] = total

    high, low = split(total)
    inner_both = dot(panel_t[...], jnp.concatenate([high, low], axis=1))
    inner_sum = inner_both[:, :chunk] + inner_both[:, chunk:]
    for index in range(n_row):
        inner[index] = inner_sum[index * piece_rows : (index + 1) * piece_rows]
    for step in range(1, n_row):
        target = lax.rem(me + step, n_row)
        remote(
            inner.at[target], inner_in.at[me], inner_send.at[step], inner_recv.at[me], target, col
        ).start()
    for step in range(1, n_col):
        target = lax.rem(col + step, n_col)
        remote(
            sums.at[col], sums.at[col], sums_send.at[step], sums_recv.at[col], me, target
        ).start()
    piece = inner[me]
    for step in range(1, n_row):
        source = lax.rem(me + step, n_row)
        remote(
            inner.at[source], inner_in.at[source], inner_send.at[step], inner_recv.at[source], source, col
        ).wait_recv()
        piece = piece + inner_in[source]
    pieces[me, col] = piece
    for step in range(1, n_col):
        target = lax.rem(col + step, n_col)
        remote(
            pieces.at[me, col], pieces.at[me, col], piece_send.at[step], piece_recv.at[col], me, target
        ).start()
    for step in range(1, n_col):
        source = lax.rem(col + step, n_col)
        remote(
            pieces.at[me, source], pieces.at[me, source], piece_send.at[step], piece_recv.at[source], me, source
        ).wait_recv()
    for step in range(1, n_chip):
        target = lax.rem(chip + step, n_chip) * 2 + core
        remote(
            pieces.at[me], pieces.at[me], row_send.at[step], row_recv.at[me], target, col
        ).start()
    remote(pieces.at[me], pieces.at[me], row_fwd.at[chip], row_recv.at[me], partner, col).start()

    for step in range(1, n_col):
        source = lax.rem(col + step, n_col)
        remote(
            sums.at[source], sums.at[source], sums_send.at[step], sums_recv.at[source], me, source
        ).wait_recv()
    full = jnp.concatenate([sums[index] for index in range(n_col)], axis=1)
    done_high, done_low = {}, {}
    for k in range(window_count - 1, -1, -1):
        value = full[:, k * block : (k + 1) * block]
        later = range(k + 1, window_count)
        if k + 1 < window_count:
            factor = jnp.concatenate(
                [factor_ref[pair_index(w, k, window_count)] for w in later], axis=0
            )
            left = jnp.concatenate(
                [
                    jnp.concatenate([done_high[w] for w in later], axis=1),
                    jnp.concatenate([done_low[w] for w in later], axis=1),
                ],
                axis=0,
            )
            term = dot(left, factor)
            value = value + (term[:rows] + term[rows:])
        value = -value
        done_high[k], done_low[k] = split(value)
        column_ref[k] = jnp.where(own_level <= k, value, 0.0)

    for step in range(1, n_chip):
        source = lax.rem(chip + step, n_chip)
        row = source * 2 + core
        forward = remote(
            pieces.at[row], pieces.at[row], row_fwd.at[source], row_recv.at[row], partner, col
        )
        forward.wait_recv()
        forward.start()
    for source in range(n_chip):
        row = source * 2 + 1 - core
        remote(
            pieces.at[row], pieces.at[row], row_fwd.at[source], row_recv.at[row], partner, col
        ).wait_recv()

    known = jnp.concatenate(
        [
            jnp.concatenate([pieces[row, index] for index in range(n_col)], axis=1)
            for row in range(n_row)
        ],
        axis=0,
    )
    for k in range(window_count - 1, -1, -1):
        start = k * block
        value = known[:, start : start + block]
        zero = jnp.zeros((block, block), F32)
        value = value + jnp.concatenate(
            [diag_ref[k] if w == k else zero for w in range(window_count)], axis=0
        )
        if k + 1 < window_count:
            factor = jnp.concatenate(
                [factor_ref[pair_index(w, k, window_count)] for w in range(k + 1, window_count)],
                axis=0,
            )
            after = pl.ds(start + block, width - start - block)
            value = value - (dot(x_parts[0, :, after], factor) + dot(x_parts[1, :, after], factor))
        high, low = split(value)
        x_parts[0, :, pl.ds(start, block)] = high
        x_parts[1, :, pl.ds(start, block)] = low
        window_ref[:, pl.ds(start, block)] = value
    for k in range(window_count - 1, -1, -1):
        start = k * block
        value = window_ref[pl.ds(start, block), :]
        if k + 1 < window_count:
            factor = jnp.concatenate(
                [factor_t[pair_index(w, k, window_count)] for w in range(k + 1, window_count)],
                axis=1,
            )
            after = pl.ds(start + block, width - start - block)
            value = value - (dot(factor, w_parts[0, after, :]) + dot(factor, w_parts[1, after, :]))
            window_ref[pl.ds(start, block), :] = value
        high, low = split(value)
        w_parts[0, pl.ds(start, block), :] = high
        w_parts[1, pl.ds(start, block), :] = low

    for turn in range(local_blocks // 2):
        mine = 2 * turn + core

        @pl.when(me == col * local_blocks + mine)
        def _():
            for step in range(1, n_chip):
                remote(
                    panel_ref, panels.at[mine], panel_send.at[turn, step], panel_recv.at[mine], partner, col
                ).wait_send()

        remote(
            panels.at[mine], panels.at[mine], panel_fwd.at[turn], panel_recv.at[mine], partner, col
        ).wait_send()
    for step in range(1, n_col):
        remote(
            product.at[col], product_in.at[col], product_send.at[step], product_recv.at[col], me, col
        ).wait_send()
        remote(sums.at[col], sums.at[col], sums_send.at[step], sums_recv.at[col], me, col).wait_send()
        remote(
            pieces.at[me, col], pieces.at[me, col], piece_send.at[step], piece_recv.at[col], me, col
        ).wait_send()
    for step in range(1, n_row):
        remote(
            inner.at[me], inner_in.at[me], inner_send.at[step], inner_recv.at[me], partner, col
        ).wait_send()
    for step in range(1, n_chip):
        remote(pieces.at[me], pieces.at[me], row_send.at[step], row_recv.at[me], partner, col).wait_send()
    for source in range(n_chip):
        remote(
            pieces.at[me], pieces.at[me], row_fwd.at[source], row_recv.at[me], partner, col
        ).wait_send()


def solution(mesh):
    n_row, n_col = mesh.shape["prow"], mesh.shape["pcol"]

    def shards(cov_trail, factor_panel, first_level, block_slot, factor_window, diag_inverse):
        window_count, block = diag_inverse.shape[0], diag_inverse.shape[-1]
        rows, cols = cov_trail.shape
        width = window_count * block
        chunk = width // n_col
        piece = width // n_row
        local_blocks = cols // block
        pairs = factor_window.shape[0]
        vmem = pl.BlockSpec(memory_space=pltpu.VMEM)
        smem = pl.BlockSpec(memory_space=pltpu.SMEM)
        dma = pltpu.SemaphoreType.DMA
        return pl.pallas_call(
            functools.partial(kernel, (n_row, n_col, window_count, block)),
            out_shape=(
                jax.ShapeDtypeStruct((window_count, rows, block), F32),
                jax.ShapeDtypeStruct((width, width), F32),
            ),
            in_specs=[smem, smem, vmem, vmem, vmem, vmem],
            out_specs=(vmem, vmem),
            scratch_shapes=[
                pltpu.VMEM((local_blocks, window_count, block, block), BF16),
                pltpu.VMEM((cols, width), BF16),
                pltpu.VMEM((width, rows), BF16),
                pltpu.VMEM((pairs, block, block), BF16),
                pltpu.VMEM((n_col, rows, chunk), F32),
                pltpu.VMEM((n_col, rows, chunk), F32),
                pltpu.VMEM((n_col, rows, chunk), F32),
                pltpu.VMEM((n_row, piece, chunk), F32),
                pltpu.VMEM((n_row, piece, chunk), F32),
                pltpu.VMEM((n_row, n_col, piece, chunk), F32),
                pltpu.VMEM((2, width, width), BF16),
                pltpu.VMEM((2, width, width), BF16),
                dma((local_blocks // 2, n_row // 2)),
                dma((local_blocks // 2,)),
                dma((local_blocks,)),
                dma((n_col,)),
                dma((n_col,)),
                dma((n_col,)),
                dma((n_col,)),
                dma((n_row,)),
                dma((n_row,)),
                dma((n_col,)),
                dma((n_col,)),
                dma((n_row // 2,)),
                dma((n_row // 2,)),
                dma((n_row,)),
            ],
            compiler_params=pltpu.CompilerParams(
                collective_id=0, has_side_effects=True, vmem_limit_bytes=40 * 1024 * 1024
            ),
        )(first_level, block_slot, cov_trail, factor_panel, factor_window, diag_inverse)

    return jax.shard_map(
        shards,
        mesh=mesh,
        in_specs=(P("prow", "pcol"), P(None, "prow", None), P(), P(), P(), P()),
        out_specs=(P(None, "prow", None), P()),
        check_vma=False,
    )
```

time: 170 us -> 48.5 us (0.29); the launches traced: 168 us -> 48.1 us
  waiting for transfers between devices: 89.7 us -> 0 us
  Pallas kernels: 0 us -> 40.8 us
  blocking collectives: 37.5 us -> 0 us
  between operations: 17.1 us -> 0.65 us
  matrix products: 13.7 us -> 0 us
  other arithmetic: 5.08 us -> 0 us
  local copies, waits for them, and re-layouts: 4.56 us -> 6.66 us
    psum x2 -> x0, waiting for transfers between devices: 89.7 us -> none  [the longest x1 55.4 us: shards(): cross_sums = lax.psum(jnp.stack(term_list), 'prow')]
    pallas_call x0 -> x1, Pallas kernels: none -> 40.8 us  [shards(): pl.pallas_call(functools.partial(kernel, (n_row, n_col, window_count, blo...]
    all_gather x4 -> x0, blocking collectives: 37.5 us -> none  [shards(): gathered = lax.all_gather(panel_row, 'prow', axis=0, tiled=True)]
    dot_general x40 -> x0, matrix products: 13.7 us -> none  [the longest x4 3.56 us: shards(): jnp.dot(cov_trail, panel_col.astype(jnp.float32), precision=highest, pref...]
    unnamed x26 -> x14, local copies, waits for them, and re-layouts: 3.41 us -> 6.66 us
    another operation x5 -> x0, other arithmetic: 2.11 us -> none  [the longest x3 2.07 us: shards(): cross_sums = lax.psum(jnp.stack(term_list), 'prow')]
  transfers between devices with their start and end apart: 2 -> 0, of which waited for: 2 -> 0; matrix products, arithmetic and copies ran while one was open for 1% -> 0% of each run, Pallas kernels for 0% -> 0%
where the time goes in v1:
time: 48.5 us; the launch traced here: 48.1 us
  Pallas kernels  40.8 us (84%)
  local copies, waits for them, and re-layouts  6.66 us (14%)
  between operations  0.65 us (1%)
    pallas_call x1, Pallas kernels, shards(): pl.pallas_call(functools.partial(kernel, (n_row, n_col, window_count, blo...  40.8 us
    unnamed x14, local copies, waits for them, and re-layouts  6.66 us

profile of v1, /device:TPU:1, one launch (start us, length us, event | category | flops | bytes accessed | tf_op | source)
XLA Modules:
  0.0 48.1 jit_solution(9861558085787670781)
XLA Ops:
  0.6 0.0 copy-start
  0.6 0.9 %copy-done = f32[4,128,128]{2,1,0:T(8,128)S(1)} copy-done((f32[4,128,128]{2,1,0:T(8,128)S(1)}, f32[4,128,128]{2,1,0:T(8,128)}, u32[]{:S(2)}) %copy-start) | copy-done | bytes 262168
  1.6 0.0 copy-start.1
  1.6 0.9 %copy-done.1 = bf16[6,128,128]{2,1,0:T(8,128)(2,1)S(1)} copy-done((bf16[6,128,128]{2,1,0:T(8,128)(2,1)S(1)}, bf16[6,128,128]{2,1,0:T(8,128)(2,1)}, u32[]{:S(2)}) %copy-start.1) | copy-done | bytes 196632
  2.5 0.0 copy-start.2
  2.5 0.9 %copy-done.2 = f32[128,256]{1,0:T(8,128)S(1)} copy-done((f32[128,256]{1,0:T(8,128)S(1)}, f32[128,256]{1,0:T(8,128)}, u32[]{:S(2)}) %copy-start.2) | copy-done | bytes 131096
  3.4 0.0 copy-start.3
  3.4 0.9 %copy-done.3 = bf16[4,128,128]{2,1,0:T(8,128)(2,1)S(1)} copy-done((bf16[4,128,128]{2,1,0:T(8,128)(2,1)S(1)}, bf16[4,128,128]{2,1,0:T(8,128)(2,1)}, u32[]{:S(2)}) %copy-start.3) | copy-done | bytes 131096
  4.3 0.0 copy-start.4
  4.3 0.7 %copy-done.4 = s32[8]{0:T(128)S(1)} copy-done((s32[8]{0:T(128)S(1)}, s32[8]{0:T(128)}, u32[]{:S(2)}) %copy-start.4) | copy-done | bytes 56
  5.0 0.0 copy-start.5
  5.0 0.7 %copy-done.5 = s32[8]{0:T(128)S(1)} copy-done((s32[8]{0:T(128)S(1)}, s32[8]{0:T(128)}, u32[]{:S(2)}) %copy-start.5) | copy-done | bytes 56
  5.6 40.8 %shard_map.77 = (f32[4,128,128]{2,1,0:T(8,128)S(1)}, f32[512,512]{1,0:T(8,128)S(1)}) custom-call(s32[8]{0:T(128)S(1)} %copy-done.4, s32[8]{0:T(128)S(1)} %copy-done.5, f32[128,256]{1,0:T(8,128)S(1)} %copy-done.2, bf16[4,128,128]{2,1,0:T(8,128)(2,1)S(1)} %copy-done.3, bf16[6,128,128]{2,1,0:T(8,128)(2,1)S(1)} %copy-done.1, f32[4,128,128]{2,1,0:T(8,128)S(1)} %copy-done), custom_call_target="tpu_custom_call" | custom-call | tf_op jit(solution)/shard_map/pallas_call | solution.py:343
  46.4 0.7 %copy.10 = f32[4,128,128]{2,1,0:T(8,128)} copy(f32[4,128,128]{2,1,0:T(8,128)S(1)} %get-tuple-element.4) | data formatting | bytes 524288
  47.1 1.0 %copy.11 = f32[512,512]{1,0:T(8,128)} copy(f32[512,512]{1,0:T(8,128)S(1)} %get-tuple-element.5) | data formatting | bytes 2097152
Async XLA Ops:
  0.6 1.0 %copy-start = (f32[4,128,128]{2,1,0:T(8,128)S(1)}, f32[4,128,128]{2,1,0:T(8,128)}, u32[]{:S(2)}) copy-start(f32[4,128,128]{2,1,0:T(8,128)} %diag_ref.1) | copy-start | bytes 786436
  1.6 0.9 %copy-start.1 = (bf16[6,128,128]{2,1,0:T(8,128)(2,1)S(1)}, bf16[6,128,128]{2,1,0:T(8,128)(2,1)}, u32[]{:S(2)}) copy-start(bf16[6,128,128]{2,1,0:T(8,128)(2,1)} %factor_ref.1) | copy-start | bytes 589828
  2.5 0.9 %copy-start.2 = (f32[128,256]{1,0:T(8,128)S(1)}, f32[128,256]{1,0:T(8,128)}, u32[]{:S(2)}) copy-start(f32[128,256]{1,0:T(8,128)} %cov_ref.1) | copy-start | bytes 393220
  3.4 0.9 %copy-start.3 = (bf16[4,128,128]{2,1,0:T(8,128)(2,1)S(1)}, bf16[4,128,128]{2,1,0:T(8,128)(2,1)}, u32[]{:S(2)}) copy-start(bf16[4,128,128]{2,1,0:T(8,128)(2,1)} %panel_ref.1) | copy-start | bytes 393220
  4.3 0.7 %copy-start.4 = (s32[8]{0:T(128)S(1)}, s32[8]{0:T(128)}, u32[]{:S(2)}) copy-start(s32[8]{0:T(128)} %first_ref.1) | copy-start | bytes 100
  5.0 0.7 %copy-start.5 = (s32[8]{0:T(128)S(1)}, s32[8]{0:T(128)}, u32[]{:S(2)}) copy-start(s32[8]{0:T(128)} %slot_ref.1) | copy-start | bytes 100

commit v2 on v1

--- a/solution.py
+++ b/solution.py
@@ -27,14 +27,21 @@
 
 def kernel(
     sizes,
+    first_hbm,
+    slot_hbm,
+    cov_hbm,
+    panel_hbm,
+    factor_hbm,
+    diag_hbm,
+    column_ref,
+    window_ref,
     first_ref,
     slot_ref,
     cov_ref,
     panel_ref,
     factor_ref,
     diag_ref,
-    column_ref,
-    window_ref,
+    load_sem,
     panels,
     masked,
     panel_t,
@@ -92,6 +99,21 @@
             level = level + jnp.where(slot_ref[index] == slot, first_ref[index], 0)
         return level
 
+    loads = [
+        pltpu.make_async_copy(source, target, load_sem.at[index])
+        for index, (source, target) in enumerate(
+            (
+                (panel_hbm, panel_ref),
+                (first_hbm, first_ref),
+                (slot_hbm, slot_ref),
+                (cov_hbm, cov_ref),
+                (factor_hbm, factor_ref),
+                (diag_hbm, diag_ref),
+            )
+        )
+    ]
+    for load in loads:
+        load.start()
     barrier = pltpu.get_barrier_semaphore()
     for step in range(1, n_row):
         pl.semaphore_signal(
@@ -102,6 +124,7 @@
             barrier, inc=1, device_id=(me, lax.rem(col + step, n_col)), device_id_type=MESH
         )
     pl.semaphore_wait(barrier, n_row + n_col - 2)
+    loads[0].wait()
 
     for turn in range(local_blocks // 2):
         mine = 2 * turn + core
@@ -119,12 +142,16 @@
             ).start()
             panels[mine] = panel_ref[...]
 
+    loads[1].wait()
+    loads[2].wait()
     own_level = level_of(me)
     for k in range(window_count):
         own = jnp.where(own_level <= k, panel_ref[k].astype(F32), 0.0)
         panel_t[pl.ds(k * block, block), :] = own.T.astype(BF16)
+    loads[4].wait()
     for index in range(factor_ref.shape[0]):
         factor_t[index] = factor_ref[index].astype(F32).T.astype(BF16)
+    loads[3].wait()
     cov_high, cov_low = split(cov_ref[...])
     cov_parts = jnp.concatenate([cov_high, cov_low], axis=0)
 
@@ -253,6 +280,7 @@
             pieces.at[row], pieces.at[row], row_fwd.at[source], row_recv.at[row], partner, col
         ).wait_recv()
 
+    loads[5].wait()
     known = jnp.concatenate(
         [
             jnp.concatenate([pieces[row, index] for index in range(n_col)], axis=1)
@@ -338,7 +366,7 @@
         local_blocks = cols // block
         pairs = factor_window.shape[0]
         vmem = pl.BlockSpec(memory_space=pltpu.VMEM)
-        smem = pl.BlockSpec(memory_space=pltpu.SMEM)
+        hbm = pl.BlockSpec(memory_space=pltpu.MemorySpace.HBM)
         dma = pltpu.SemaphoreType.DMA
         return pl.pallas_call(
             functools.partial(kernel, (n_row, n_col, window_count, block)),
@@ -346,9 +374,16 @@
                 jax.ShapeDtypeStruct((window_count, rows, block), F32),
                 jax.ShapeDtypeStruct((width, width), F32),
             ),
-            in_specs=[smem, smem, vmem, vmem, vmem, vmem],
+            in_specs=[hbm] * 6,
             out_specs=(vmem, vmem),
             scratch_shapes=[
+                pltpu.SMEM(first_level.shape, jnp.int32),
+                pltpu.SMEM(block_slot.shape, jnp.int32),
+                pltpu.VMEM(cov_trail.shape, F32),
+                pltpu.VMEM(factor_panel.shape, BF16),
+                pltpu.VMEM(factor_window.shape, BF16),
+                pltpu.VMEM(diag_inverse.shape, F32),
+                dma((6,)),
                 pltpu.VMEM((local_blocks, window_count, block, block), BF16),
                 pltpu.VMEM((cols, width), BF16),
                 pltpu.VMEM((width, rows), BF16),
@@ -377,7 +412,7 @@
                 dma((n_row,)),
             ],
             compiler_params=pltpu.CompilerParams(
-                collective_id=0, has_side_effects=True, vmem_limit_bytes=40 * 1024 * 1024
+                collective_id=0, has_side_effects=True, vmem_limit_bytes=60 * 1024 * 1024
             ),
         )(first_level, block_slot, cov_trail, factor_panel, factor_window, diag_inverse)
 

time: 48.5 us -> 45.9 us (0.946)
  local copies, waits for them, and re-layouts: 6.66 us -> 3.93 us
    unnamed x14 -> x2, local copies, waits for them, and re-layouts: 6.66 us -> 3.93 us
where the time goes in v2:
time: 45.9 us; the launch traced here: 45.7 us
  Pallas kernels  41.1 us (90%)
  local copies, waits for them, and re-layouts  3.93 us (9%)
  between operations  0.64 us (1%)
    pallas_call x1, Pallas kernels, shards(): pl.pallas_call(functools.partial(kernel, (n_row, n_col, window_count, blo...  41.1 us
    unnamed x2, local copies, waits for them, and re-layouts  3.93 us

profile of v2, /device:TPU:1, one launch (start us, length us, event | category | flops | bytes accessed | tf_op | source)
XLA Modules:
  0.0 45.7 jit_solution(10871750620899756636)
XLA Ops:
  0.6 41.1 %shard_map.77 = (f32[4,128,128]{2,1,0:T(8,128)}, f32[512,512]{1,0:T(8,128)}) custom-call(s32[8]{0:T(128)} %first_hbm.1, s32[8]{0:T(128)} %slot_hbm.1, f32[128,256]{1,0:T(8,128)} %cov_hbm.1, bf16[4,128,128]{2,1,0:T(8,128)(2,1)} %panel_hbm.1, bf16[6,128,128]{2,1,0:T(8,128)(2,1)} %factor_hbm.1, f32[4,128,128]{2,1,0:T(8,128)} %diag_hbm.1), custom_call_target="tpu_custom_call" | custom-call | tf_op jit(solution)/shard_map/pallas_call | solution.py:371
  41.8 1.7 %copy.10 = f32[4,128,128]{2,1,0:T(8,128)} copy(f32[4,128,128]{2,1,0:T(8,128)} %get-tuple-element.4) | data formatting | bytes 524288
  43.5 2.3 %copy.11 = f32[512,512]{1,0:T(8,128)} copy(f32[512,512]{1,0:T(8,128)} %get-tuple-element.5) | data formatting | bytes 2097152

commit v3 on v2

--- a/solution.py
+++ b/solution.py
@@ -126,21 +126,30 @@
     pl.semaphore_wait(barrier, n_row + n_col - 2)
     loads[0].wait()
 
-    for turn in range(local_blocks // 2):
-        mine = 2 * turn + core
-        owner = col * local_blocks + mine
-
-        @pl.when(me == owner)
-        def _():
-            for step in range(1, n_chip):
-                target = lax.rem(chip + step, n_chip) * 2 + core
-                remote(
-                    panel_ref, panels.at[mine], panel_send.at[turn, step], panel_recv.at[mine], target, col
-                ).start()
-            remote(
-                panel_ref, panels.at[mine], panel_fwd.at[turn], panel_recv.at[mine], partner, col
-            ).start()
-            panels[mine] = panel_ref[...]
+    def panel_copy(src, mine, k, sems, index, row):
+        return remote(src.at[k], panels.at[mine, k], sems.at[index], panel_recv.at[mine, k], row, col)
+
+    def other_chips(origin):
+        if n_chip == 4:
+            side = origin + 1 - 2 * lax.rem(origin, 2)
+            return [side, lax.rem(origin + 2, 4)]
+        return [lax.rem(origin + step, n_chip) for step in range(1, n_chip)]
+
+    def relay_chip(origin):
+        side = origin + 1 - 2 * lax.rem(origin, 2)
+        return jnp.where(core == 0, side, lax.rem(origin + 2, 4))
+
+    order = range(window_count)
+    for k in order:
+        for turn in range(local_blocks // 2):
+            mine = 2 * turn + core
+
+            @pl.when(me == col * local_blocks + mine)
+            def _():
+                for step, target in enumerate(other_chips(chip)):
+                    panel_copy(panel_ref, mine, k, panel_send, (turn, k, step), target * 2 + core).start()
+                panel_copy(panel_ref, mine, k, panel_fwd, (turn, k), partner).start()
+                panels[mine, k] = panel_ref[k]
 
     loads[1].wait()
     loads[2].wait()
@@ -155,49 +164,65 @@
     cov_high, cov_low = split(cov_ref[...])
     cov_parts = jnp.concatenate([cov_high, cov_low], axis=0)
 
-    for turn in range(local_blocks // 2):
-        mine = 2 * turn + core
-        owner = col * local_blocks + mine
-
-        @pl.when(me != owner)
-        def _():
-            forward = remote(
-                panels.at[mine], panels.at[mine], panel_fwd.at[turn], panel_recv.at[mine], partner, col
-            )
-            forward.wait_recv()
-            forward.start()
-
-    for turn in range(local_blocks // 2):
-        other = 2 * turn + 1 - core
-        remote(
-            panels.at[other], panels.at[other], panel_fwd.at[turn], panel_recv.at[other], partner, col
-        ).wait_recv()
-
-    for index in range(local_blocks):
-        level = level_of(col * local_blocks + index)
-        for k in range(window_count):
-            masked[pl.ds(index * block, block), pl.ds(k * block, block)] = jnp.where(
-                level <= k, panels[index, k].astype(F32), 0.0
+    rows = cov_ref.shape[0]
+    levels = [level_of(col * local_blocks + index) for index in range(local_blocks)]
+    per_block = block // chunk
+    for k in order:
+        for turn in range(local_blocks // 2):
+            mine = 2 * turn + core
+            owner = col * local_blocks + mine
+            owner_chip = owner // 2
+
+            @pl.when(me != owner)
+            def _():
+                forward = panel_copy(panels.at[mine], mine, k, panel_fwd, (turn, k), partner)
+                forward.wait_recv()
+                forward.start()
+                if n_chip == 4:
+
+                    @pl.when(chip == relay_chip(owner_chip))
+                    def _():
+                        panel_copy(
+                            panels.at[mine], mine, k, panel_send, (turn, k, 0), (3 - owner_chip) * 2 + core
+                        ).start()
+
+        for turn in range(local_blocks // 2):
+            other = 2 * turn + 1 - core
+            panel_copy(panels.at[other], other, k, panel_fwd, (turn, k), partner).wait_recv()
+        for index in range(local_blocks):
+            masked[pl.ds(index * block, block), :] = jnp.where(
+                levels[index] <= k, panels[index, k].astype(F32), 0.0
             ).astype(BF16)
-
-    rows = cov_ref.shape[0]
-    both = dot(cov_parts, masked[...])
-    partial = both[:rows] + both[rows:]
-    for index in range(n_col):
-        product[index] = partial[:, index * chunk : (index + 1) * chunk]
-    for step in range(1, n_col):
-        target = lax.rem(col + step, n_col)
-        remote(
-            product.at[target], product_in.at[col], product_send.at[step], product_recv.at[col], me, target
-        ).start()
+        both = dot(cov_parts, masked[...])
+        partial = both[:rows] + both[rows:]
+        for part in range(per_block):
+            target = k * per_block + part
+            product[target] = partial[:, part * chunk : (part + 1) * chunk]
+
+            @pl.when(col != target)
+            def _():
+                remote(
+                    product.at[target],
+                    product_in.at[col],
+                    product_send.at[target],
+                    product_recv.at[col],
+                    me,
+                    target,
+                ).start()
+
     total = product[col]
     for step in range(1, n_col):
         source = lax.rem(col + step, n_col)
         remote(
-            product.at[source], product_in.at[source], product_send.at[step], product_recv.at[source], me, source
+            product.at[source], product_in.at[source], product_send.at[source], product_recv.at[source], me, source
         ).wait_recv()
         total = total + product_in[source]
     sums[col] = total
+
+    def sums_copy(source, way, distance, target):
+        return remote(
+            sums.at[source], sums.at[source], sums_send.at[way, distance], sums_recv.at[source], me, target
+        )
 
     high, low = split(total)
     inner_both = dot(panel_t[...], jnp.concatenate([high, low], axis=1))
@@ -209,11 +234,36 @@
         remote(
             inner.at[target], inner_in.at[me], inner_send.at[step], inner_recv.at[me], target, col
         ).start()
-    for step in range(1, n_col):
-        target = lax.rem(col + step, n_col)
-        remote(
-            sums.at[col], sums.at[col], sums_send.at[step], sums_recv.at[col], me, target
-        ).start()
+    def hop(distance):
+        if distance == 0:
+
+            @pl.when(col + 1 < n_col)
+            def _():
+                sums_copy(col, 0, 0, col + 1).start()
+
+            @pl.when(col > 0)
+            def _():
+                sums_copy(col, 1, 0, col - 1).start()
+
+            return
+
+        @pl.when(col >= distance)
+        def _():
+            sums_copy(col - distance, 0, distance, col).wait_recv()
+
+            @pl.when(col + 1 < n_col)
+            def _():
+                sums_copy(col - distance, 0, distance, col + 1).start()
+
+        @pl.when(col + distance < n_col)
+        def _():
+            sums_copy(col + distance, 1, distance, col).wait_recv()
+
+            @pl.when(col > 0)
+            def _():
+                sums_copy(col + distance, 1, distance, col - 1).start()
+
+    hop(0)
     piece = inner[me]
     for step in range(1, n_row):
         source = lax.rem(me + step, n_row)
@@ -227,6 +277,7 @@
         remote(
             pieces.at[me, col], pieces.at[me, col], piece_send.at[step], piece_recv.at[col], me, target
         ).start()
+    hop(1)
     for step in range(1, n_col):
         source = lax.rem(col + step, n_col)
         remote(
@@ -239,11 +290,8 @@
         ).start()
     remote(pieces.at[me], pieces.at[me], row_fwd.at[chip], row_recv.at[me], partner, col).start()
 
-    for step in range(1, n_col):
-        source = lax.rem(col + step, n_col)
-        remote(
-            sums.at[source], sums.at[source], sums_send.at[step], sums_recv.at[source], me, source
-        ).wait_recv()
+    for distance in range(2, n_col):
+        hop(distance)
     full = jnp.concatenate([sums[index] for index in range(n_col)], axis=1)
     done_high, done_low = {}, {}
     for k in range(window_count - 1, -1, -1):
@@ -321,24 +369,42 @@
         w_parts[0, pl.ds(start, block), :] = high
         w_parts[1, pl.ds(start, block), :] = low
 
-    for turn in range(local_blocks // 2):
-        mine = 2 * turn + core
-
-        @pl.when(me == col * local_blocks + mine)
+    for k in order:
+        for turn in range(local_blocks // 2):
+            mine = 2 * turn + core
+            owner = col * local_blocks + mine
+
+            @pl.when(me == owner)
+            def _():
+                for step, target in enumerate(other_chips(chip)):
+                    panel_copy(panel_ref, mine, k, panel_send, (turn, k, step), target * 2 + core).wait_send()
+
+            if n_chip == 4:
+
+                @pl.when((me != owner) & (chip == relay_chip(owner // 2)))
+                def _():
+                    panel_copy(panel_ref, mine, k, panel_send, (turn, k, 0), partner).wait_send()
+
+            panel_copy(panel_ref, mine, k, panel_fwd, (turn, k), partner).wait_send()
+    for target in range(n_col):
+
+        @pl.when(col != target)
         def _():
-            for step in range(1, n_chip):
-                remote(
-                    panel_ref, panels.at[mine], panel_send.at[turn, step], panel_recv.at[mine], partner, col
-                ).wait_send()
-
-        remote(
-            panels.at[mine], panels.at[mine], panel_fwd.at[turn], panel_recv.at[mine], partner, col
-        ).wait_send()
+            remote(
+                product.at[target], product_in.at[col], product_send.at[target], product_recv.at[col], me, target
+            ).wait_send()
+
+    for distance in range(n_col):
+
+        @pl.when((col >= distance) & (col + 1 < n_col))
+        def _():
+            sums_copy(col, 0, distance, col + 1).wait_send()
+
+        @pl.when((col + distance < n_col) & (col > 0))
+        def _():
+            sums_copy(col, 1, distance, col - 1).wait_send()
+
     for step in range(1, n_col):
-        remote(
-            product.at[col], product_in.at[col], product_send.at[step], product_recv.at[col], me, col
-        ).wait_send()
-        remote(sums.at[col], sums.at[col], sums_send.at[step], sums_recv.at[col], me, col).wait_send()
         remote(
             pieces.at[me, col], pieces.at[me, col], piece_send.at[step], piece_recv.at[col], me, col
         ).wait_send()
@@ -385,7 +451,7 @@
                 pltpu.VMEM(diag_inverse.shape, F32),
                 dma((6,)),
                 pltpu.VMEM((local_blocks, window_count, block, block), BF16),
-                pltpu.VMEM((cols, width), BF16),
+                pltpu.VMEM((cols, block), BF16),
                 pltpu.VMEM((width, rows), BF16),
                 pltpu.VMEM((pairs, block, block), BF16),
                 pltpu.VMEM((n_col, rows, chunk), F32),
@@ -396,12 +462,12 @@
                 pltpu.VMEM((n_row, n_col, piece, chunk), F32),
                 pltpu.VMEM((2, width, width), BF16),
                 pltpu.VMEM((2, width, width), BF16),
-                dma((local_blocks // 2, n_row // 2)),
-                dma((local_blocks // 2,)),
-                dma((local_blocks,)),
+                dma((local_blocks // 2, window_count, n_row // 2)),
+                dma((local_blocks // 2, window_count)),
+                dma((local_blocks, window_count)),
                 dma((n_col,)),
                 dma((n_col,)),
-                dma((n_col,)),
+                dma((2, n_col)),
                 dma((n_col,)),
                 dma((n_row,)),
                 dma((n_row,)),

time: 45.9 us -> 46.6 us (1.015)
  Pallas kernels: 41.1 us -> 41.8 us
    pallas_call x1, Pallas kernels: 41.1 us -> 41.8 us  [shards(): pl.pallas_call(functools.partial(kernel, (n_row, n_col, window_count, blo...]
where the time goes in v3:
time: 46.6 us; the launch traced here: 46.4 us
  Pallas kernels  41.8 us (90%)
  local copies, waits for them, and re-layouts  3.93 us (8%)
  between operations  0.64 us (1%)
    pallas_call x1, Pallas kernels, shards(): pl.pallas_call(functools.partial(kernel, (n_row, n_col, window_count, blo...  41.8 us
    unnamed x2, local copies, waits for them, and re-layouts  3.93 us

profile of v3, /device:TPU:1, one launch (start us, length us, event | category | flops | bytes accessed | tf_op | source)
XLA Modules:
  0.0 46.4 jit_solution(18104868025211824126)
XLA Ops:
  0.6 41.8 %shard_map.77 = (f32[4,128,128]{2,1,0:T(8,128)}, f32[512,512]{1,0:T(8,128)}) custom-call(s32[8]{0:T(128)} %first_hbm.1, s32[8]{0:T(128)} %slot_hbm.1, f32[128,256]{1,0:T(8,128)} %cov_hbm.1, bf16[4,128,128]{2,1,0:T(8,128)(2,1)} %panel_hbm.1, bf16[6,128,128]{2,1,0:T(8,128)(2,1)} %factor_hbm.1, f32[4,128,128]{2,1,0:T(8,128)} %diag_hbm.1), custom_call_target="tpu_custom_call" | custom-call | tf_op jit(solution)/shard_map/pallas_call | solution.py:437
  42.4 1.7 %copy.10 = f32[4,128,128]{2,1,0:T(8,128)} copy(f32[4,128,128]{2,1,0:T(8,128)} %get-tuple-element.4) | data formatting | bytes 524288
  44.1 2.3 %copy.11 = f32[512,512]{1,0:T(8,128)} copy(f32[512,512]{1,0:T(8,128)} %get-tuple-element.5) | data formatting | bytes 2097152

commit v4 on v3

--- a/solution.py
+++ b/solution.py
@@ -76,7 +76,8 @@
     block_count = first_ref.shape[0]
     row_blocks = cov_ref.shape[0] // block
     chunk = product.shape[2]
-    piece_rows = width // n_row
+    piece_rows = pieces.shape[2]
+    keep = piece_rows * n_row // block
     me = lax.axis_index("prow")
     col = lax.axis_index("pcol")
     core = lax.rem(me, 2)
@@ -225,7 +226,15 @@
         )
 
     high, low = split(total)
-    inner_both = dot(panel_t[...], jnp.concatenate([high, low], axis=1))
+    first = col * window_count // n_col
+    kept = jnp.concatenate(
+        [
+            panel_t[pl.ds(pl.multiple_of(lax.rem(first + t, window_count) * block, block), block), :]
+            for t in range(keep)
+        ],
+        axis=0,
+    )
+    inner_both = dot(kept, jnp.concatenate([high, low], axis=1))
     inner_sum = inner_both[:, :chunk] + inner_both[:, chunk:]
     for index in range(n_row):
         inner[index] = inner_sum[index * piece_rows : (index + 1) * piece_rows]
@@ -234,36 +243,16 @@
         remote(
             inner.at[target], inner_in.at[me], inner_send.at[step], inner_recv.at[me], target, col
         ).start()
-    def hop(distance):
-        if distance == 0:
-
-            @pl.when(col + 1 < n_col)
-            def _():
-                sums_copy(col, 0, 0, col + 1).start()
-
-            @pl.when(col > 0)
-            def _():
-                sums_copy(col, 1, 0, col - 1).start()
-
-            return
+    def send_sums(distance):
+        @pl.when(col + distance < n_col)
+        def _():
+            sums_copy(col, 0, distance, col + distance).start()
 
         @pl.when(col >= distance)
         def _():
-            sums_copy(col - distance, 0, distance, col).wait_recv()
-
-            @pl.when(col + 1 < n_col)
-            def _():
-                sums_copy(col - distance, 0, distance, col + 1).start()
-
-        @pl.when(col + distance < n_col)
-        def _():
-            sums_copy(col + distance, 1, distance, col).wait_recv()
-
-            @pl.when(col > 0)
-            def _():
-                sums_copy(col + distance, 1, distance, col - 1).start()
-
-    hop(0)
+            sums_copy(col, 1, distance, col - distance).start()
+
+    send_sums(1)
     piece = inner[me]
     for step in range(1, n_row):
         source = lax.rem(me + step, n_row)
@@ -277,7 +266,6 @@
         remote(
             pieces.at[me, col], pieces.at[me, col], piece_send.at[step], piece_recv.at[col], me, target
         ).start()
-    hop(1)
     for step in range(1, n_col):
         source = lax.rem(col + step, n_col)
         remote(
@@ -291,7 +279,18 @@
     remote(pieces.at[me], pieces.at[me], row_fwd.at[chip], row_recv.at[me], partner, col).start()
 
     for distance in range(2, n_col):
-        hop(distance)
+        send_sums(distance)
+    for step in range(1, n_chip):
+        source = lax.rem(chip + step, n_chip)
+        row = source * 2 + core
+        forward = remote(
+            pieces.at[row], pieces.at[row], row_fwd.at[source], row_recv.at[row], partner, col
+        )
+        forward.wait_recv()
+        forward.start()
+    for step in range(1, n_col):
+        source = lax.rem(col + step, n_col)
+        sums_copy(source, 0, 0, col).wait_recv()
     full = jnp.concatenate([sums[index] for index in range(n_col)], axis=1)
     done_high, done_low = {}, {}
     for k in range(window_count - 1, -1, -1):
@@ -314,14 +313,6 @@
         done_high[k], done_low[k] = split(value)
         column_ref[k] = jnp.where(own_level <= k, value, 0.0)
 
-    for step in range(1, n_chip):
-        source = lax.rem(chip + step, n_chip)
-        row = source * 2 + core
-        forward = remote(
-            pieces.at[row], pieces.at[row], row_fwd.at[source], row_recv.at[row], partner, col
-        )
-        forward.wait_recv()
-        forward.start()
     for source in range(n_chip):
         row = source * 2 + 1 - core
         remote(
@@ -329,16 +320,24 @@
         ).wait_recv()
 
     loads[5].wait()
-    known = jnp.concatenate(
-        [
-            jnp.concatenate([pieces[row, index] for index in range(n_col)], axis=1)
-            for row in range(n_row)
-        ],
-        axis=0,
-    )
+    given = {}
+    for k in range(window_count):
+        stack = jnp.concatenate(
+            [
+                jnp.concatenate(
+                    [pieces[row, k * per_block + part] for part in range(per_block)], axis=1
+                )
+                for row in range(n_row)
+            ],
+            axis=0,
+        )
+        for t in range(keep):
+            given[(k + t) % window_count, k] = stack[t * block : (t + 1) * block]
     for k in range(window_count - 1, -1, -1):
         start = k * block
-        value = known[:, start : start + block]
+        value = jnp.concatenate(
+            [given[w, k] if (w, k) in given else given[k, w].T for w in range(window_count)], axis=0
+        )
         zero = jnp.zeros((block, block), F32)
         value = value + jnp.concatenate(
             [diag_ref[k] if w == k else zero for w in range(window_count)], axis=0
@@ -394,15 +393,15 @@
                 product.at[target], product_in.at[col], product_send.at[target], product_recv.at[col], me, target
             ).wait_send()
 
-    for distance in range(n_col):
-
-        @pl.when((col >= distance) & (col + 1 < n_col))
+    for distance in range(1, n_col):
+
+        @pl.when(col + distance < n_col)
         def _():
-            sums_copy(col, 0, distance, col + 1).wait_send()
-
-        @pl.when((col + distance < n_col) & (col > 0))
+            sums_copy(col, 0, distance, col + distance).wait_send()
+
+        @pl.when(col >= distance)
         def _():
-            sums_copy(col, 1, distance, col - 1).wait_send()
+            sums_copy(col, 1, distance, col - distance).wait_send()
 
     for step in range(1, n_col):
         remote(
@@ -428,7 +427,8 @@
         rows, cols = cov_trail.shape
         width = window_count * block
         chunk = width // n_col
-        piece = width // n_row
+        kept = (window_count // 2 + 1) * block
+        piece = (kept if kept % (8 * n_row) == 0 else width) // n_row
         local_blocks = cols // block
         pairs = factor_window.shape[0]
         vmem = pl.BlockSpec(memory_space=pltpu.VMEM)

time: 46.6 us -> 43.6 us (0.936)
  Pallas kernels: 41.8 us -> 38.9 us
    pallas_call x1, Pallas kernels: 41.8 us -> 38.9 us  [shards(): pl.pallas_call(functools.partial(kernel, (n_row, n_col, window_count, blo...]
where the time goes in v4:
time: 43.6 us; the launch traced here: 43.4 us
  Pallas kernels  38.9 us (89%)
  local copies, waits for them, and re-layouts  3.93 us (9%)
  between operations  0.64 us (1%)
    pallas_call x1, Pallas kernels, shards(): pl.pallas_call(functools.partial(kernel, (n_row, n_col, window_count, blo...  38.9 us
    unnamed x2, local copies, waits for them, and re-layouts  3.93 us

profile of v4, /device:TPU:1, one launch (start us, length us, event | category | flops | bytes accessed | tf_op | source)
XLA Modules:
  0.0 43.4 jit_solution(15679567016063807171)
XLA Ops:
  0.6 38.9 %shard_map.77 = (f32[4,128,128]{2,1,0:T(8,128)}, f32[512,512]{1,0:T(8,128)}) custom-call(s32[8]{0:T(128)} %first_hbm.1, s32[8]{0:T(128)} %slot_hbm.1, f32[128,256]{1,0:T(8,128)} %cov_hbm.1, bf16[4,128,128]{2,1,0:T(8,128)(2,1)} %panel_hbm.1, bf16[6,128,128]{2,1,0:T(8,128)(2,1)} %factor_hbm.1, f32[4,128,128]{2,1,0:T(8,128)} %diag_hbm.1), custom_call_target="tpu_custom_call" | custom-call | tf_op jit(solution)/shard_map/pallas_call | solution.py:437
  39.5 1.7 %copy.10 = f32[4,128,128]{2,1,0:T(8,128)} copy(f32[4,128,128]{2,1,0:T(8,128)} %get-tuple-element.4) | data formatting | bytes 524288
  41.2 2.3 %copy.11 = f32[512,512]{1,0:T(8,128)} copy(f32[512,512]{1,0:T(8,128)} %get-tuple-element.5) | data formatting | bytes 2097152

commit v5 on v4

--- a/solution.py
+++ b/solution.py
@@ -266,28 +266,29 @@
         remote(
             pieces.at[me, col], pieces.at[me, col], piece_send.at[step], piece_recv.at[col], me, target
         ).start()
-    for step in range(1, n_col):
-        source = lax.rem(col + step, n_col)
-        remote(
-            pieces.at[me, source], pieces.at[me, source], piece_send.at[step], piece_recv.at[source], me, source
-        ).wait_recv()
-    for step in range(1, n_chip):
-        target = lax.rem(chip + step, n_chip) * 2 + core
-        remote(
-            pieces.at[me], pieces.at[me], row_send.at[step], row_recv.at[me], target, col
-        ).start()
-    remote(pieces.at[me], pieces.at[me], row_fwd.at[chip], row_recv.at[me], partner, col).start()
-
+    def row_copy(row, index, sems, slot, target):
+        return remote(
+            pieces.at[row, index], pieces.at[row, index], sems.at[slot, index], row_recv.at[row, index], target, col
+        )
+
+    for turn in range(n_col):
+        index = lax.rem(col + turn, n_col)
+        if turn:
+            remote(
+                pieces.at[me, index], pieces.at[me, index], piece_send.at[turn], piece_recv.at[index], me, index
+            ).wait_recv()
+        for step in range(1, n_chip):
+            row_copy(me, index, row_send, step, lax.rem(chip + step, n_chip) * 2 + core).start()
+        row_copy(me, index, row_fwd, chip, partner).start()
     for distance in range(2, n_col):
         send_sums(distance)
-    for step in range(1, n_chip):
-        source = lax.rem(chip + step, n_chip)
-        row = source * 2 + core
-        forward = remote(
-            pieces.at[row], pieces.at[row], row_fwd.at[source], row_recv.at[row], partner, col
-        )
-        forward.wait_recv()
-        forward.start()
+    for turn in range(n_col):
+        index = lax.rem(col + turn, n_col)
+        for step in range(1, n_chip):
+            source = lax.rem(chip + step, n_chip)
+            forward = row_copy(source * 2 + core, index, row_fwd, source, partner)
+            forward.wait_recv()
+            forward.start()
     for step in range(1, n_col):
         source = lax.rem(col + step, n_col)
         sums_copy(source, 0, 0, col).wait_recv()
@@ -314,10 +315,8 @@
         column_ref[k] = jnp.where(own_level <= k, value, 0.0)
 
     for source in range(n_chip):
-        row = source * 2 + 1 - core
-        remote(
-            pieces.at[row], pieces.at[row], row_fwd.at[source], row_recv.at[row], partner, col
-        ).wait_recv()
+        for index in range(n_col):
+            row_copy(source * 2 + 1 - core, index, row_fwd, source, partner).wait_recv()
 
     loads[5].wait()
     given = {}
@@ -411,12 +410,11 @@
         remote(
             inner.at[me], inner_in.at[me], inner_send.at[step], inner_recv.at[me], partner, col
         ).wait_send()
-    for step in range(1, n_chip):
-        remote(pieces.at[me], pieces.at[me], row_send.at[step], row_recv.at[me], partner, col).wait_send()
-    for source in range(n_chip):
-        remote(
-            pieces.at[me], pieces.at[me], row_fwd.at[source], row_recv.at[me], partner, col
-        ).wait_send()
+    for index in range(n_col):
+        for step in range(1, n_chip):
+            row_copy(me, index, row_send, step, partner).wait_send()
+        for source in range(n_chip):
+            row_copy(me, index, row_fwd, source, partner).wait_send()
 
 
 def solution(mesh):
@@ -473,14 +471,19 @@
                 dma((n_row,)),
                 dma((n_col,)),
                 dma((n_col,)),
-                dma((n_row // 2,)),
-                dma((n_row // 2,)),
-                dma((n_row,)),
+                dma((n_row // 2, n_col)),
+                dma((n_row // 2, n_col)),
+                dma((n_row, n_col)),
             ],
             compiler_params=pltpu.CompilerParams(
-                collective_id=0, has_side_effects=True, vmem_limit_bytes=60 * 1024 * 1024
+                collective_id=0, has_side_effects=True, vmem_limit_bytes=40 * 1024 * 1024
             ),
-        )(first_level, block_slot, cov_trail, factor_panel, factor_window, diag_inverse)
+        )(
+            *(
+                pltpu.with_memory_space_constraint(value, pltpu.MemorySpace.HBM)
+                for value in (first_level, block_slot, cov_trail, factor_panel, factor_window, diag_inverse)
+            )
+        )
 
     return jax.shard_map(
         shards,

time: 43.6 us -> 39.3 us (0.901)
  Pallas kernels: 38.9 us -> 36.4 us
  local copies, waits for them, and re-layouts: 3.93 us -> 1.67 us
    pallas_call x1, Pallas kernels: 38.9 us -> 36.4 us  [shards(): pl.pallas_call(functools.partial(kernel, (n_row, n_col, window_count, blo...]
    unnamed x2, local copies, waits for them, and re-layouts: 3.93 us -> 1.67 us
where the time goes in v5:
time: 39.3 us; the launch traced here: 38.7 us
  Pallas kernels  36.4 us (93%)
  local copies, waits for them, and re-layouts  1.67 us (4%)
  between operations  0.64 us (2%)
    pallas_call x1, Pallas kernels, shards(): pl.pallas_call(functools.partial(kernel, (n_row, n_col, window_count, blo...  36.4 us
    unnamed x2, local copies, waits for them, and re-layouts  1.67 us

profile of v5, /device:TPU:1, one launch (start us, length us, event | category | flops | bytes accessed | tf_op | source)
XLA Modules:
  0.0 38.7 jit_solution(11498966777778577028)
XLA Ops:
  0.6 36.4 %shard_map.77 = (f32[4,128,128]{2,1,0:T(8,128)S(1)}, f32[512,512]{1,0:T(8,128)S(1)}) custom-call(s32[8]{0:T(128)} %first_hbm.1, s32[8]{0:T(128)} %slot_hbm.1, f32[128,256]{1,0:T(8,128)} %cov_hbm.1, bf16[4,128,128]{2,1,0:T(8,128)(2,1)} %panel_hbm.1, bf16[6,128,128]{2,1,0:T(8,128)(2,1)} %factor_hbm.1, f32[4,128,128]{2,1,0:T(8,128)} %diag_hbm.1), custom_call_target="tpu_custom_call" | custom-call | tf_op jit(solution)/shard_map/pallas_call | solution.py:435
  37.1 0.7 %copy.10 = f32[4,128,128]{2,1,0:T(8,128)} copy(f32[4,128,128]{2,1,0:T(8,128)S(1)} %get-tuple-element.4) | data formatting | bytes 524288
  37.8 1.0 %copy.11 = f32[512,512]{1,0:T(8,128)} copy(f32[512,512]{1,0:T(8,128)S(1)} %get-tuple-element.5) | data formatting | bytes 2097152

commit v6 on v5

--- a/solution.py
+++ b/solution.py
@@ -168,7 +168,7 @@
     rows = cov_ref.shape[0]
     levels = [level_of(col * local_blocks + index) for index in range(local_blocks)]
     per_block = block // chunk
-    for k in order:
+    def arrive(k):
         for turn in range(local_blocks // 2):
             mine = 2 * turn + core
             owner = col * local_blocks + mine
@@ -187,6 +187,7 @@
                             panels.at[mine], mine, k, panel_send, (turn, k, 0), (3 - owner_chip) * 2 + core
                         ).start()
 
+    def multiply(k):
         for turn in range(local_blocks // 2):
             other = 2 * turn + 1 - core
             panel_copy(panels.at[other], other, k, panel_fwd, (turn, k), partner).wait_recv()
@@ -210,6 +211,12 @@
                     me,
                     target,
                 ).start()
+
+    arrive(0)
+    for k in order:
+        if k + 1 < window_count:
+            arrive(k + 1)
+        multiply(k)
 
     total = product[col]
     for step in range(1, n_col):

time: 39.3 us -> 39.3 us (level)
  no operation moved by 1% of the time
where the time goes in v6:
time: 39.3 us; the launch traced here: 38.7 us
  Pallas kernels  36.3 us (92%)
  local copies, waits for them, and re-layouts  1.67 us (4%)
  between operations  0.64 us (2%)
    pallas_call x1, Pallas kernels, shards(): pl.pallas_call(functools.partial(kernel, (n_row, n_col, window_count, blo...  36.3 us
    unnamed x2, local copies, waits for them, and re-layouts  1.67 us

profile of v6, /device:TPU:1, one launch (start us, length us, event | category | flops | bytes accessed | tf_op | source)
XLA Modules:
  0.0 38.7 jit_solution(16275071842131679925)
XLA Ops:
  0.6 36.3 %shard_map.77 = (f32[4,128,128]{2,1,0:T(8,128)S(1)}, f32[512,512]{1,0:T(8,128)S(1)}) custom-call(s32[8]{0:T(128)} %first_hbm.1, s32[8]{0:T(128)} %slot_hbm.1, f32[128,256]{1,0:T(8,128)} %cov_hbm.1, bf16[4,128,128]{2,1,0:T(8,128)(2,1)} %panel_hbm.1, bf16[6,128,128]{2,1,0:T(8,128)(2,1)} %factor_hbm.1, f32[4,128,128]{2,1,0:T(8,128)} %diag_hbm.1), custom_call_target="tpu_custom_call" | custom-call | tf_op jit(solution)/shard_map/pallas_call | solution.py:442
  37.0 0.7 %copy.10 = f32[4,128,128]{2,1,0:T(8,128)} copy(f32[4,128,128]{2,1,0:T(8,128)S(1)} %get-tuple-element.4) | data formatting | bytes 524288
  37.7 1.0 %copy.11 = f32[512,512]{1,0:T(8,128)} copy(f32[512,512]{1,0:T(8,128)S(1)} %get-tuple-element.5) | data formatting | bytes 2097152

commit v7 on v6

--- a/solution.py
+++ b/solution.py
@@ -131,14 +131,7 @@
         return remote(src.at[k], panels.at[mine, k], sems.at[index], panel_recv.at[mine, k], row, col)
 
     def other_chips(origin):
-        if n_chip == 4:
-            side = origin + 1 - 2 * lax.rem(origin, 2)
-            return [side, lax.rem(origin + 2, 4)]
         return [lax.rem(origin + step, n_chip) for step in range(1, n_chip)]
-
-    def relay_chip(origin):
-        side = origin + 1 - 2 * lax.rem(origin, 2)
-        return jnp.where(core == 0, side, lax.rem(origin + 2, 4))
 
     order = range(window_count)
     for k in order:
@@ -172,20 +165,12 @@
         for turn in range(local_blocks // 2):
             mine = 2 * turn + core
             owner = col * local_blocks + mine
-            owner_chip = owner // 2
 
             @pl.when(me != owner)
             def _():
                 forward = panel_copy(panels.at[mine], mine, k, panel_fwd, (turn, k), partner)
                 forward.wait_recv()
                 forward.start()
-                if n_chip == 4:
-
-                    @pl.when(chip == relay_chip(owner_chip))
-                    def _():
-                        panel_copy(
-                            panels.at[mine], mine, k, panel_send, (turn, k, 0), (3 - owner_chip) * 2 + core
-                        ).start()
 
     def multiply(k):
         for turn in range(local_blocks // 2):
@@ -383,12 +368,6 @@
             def _():
                 for step, target in enumerate(other_chips(chip)):
                     panel_copy(panel_ref, mine, k, panel_send, (turn, k, step), target * 2 + core).wait_send()
-
-            if n_chip == 4:
-
-                @pl.when((me != owner) & (chip == relay_chip(owner // 2)))
-                def _():
-                    panel_copy(panel_ref, mine, k, panel_send, (turn, k, 0), partner).wait_send()
 
             panel_copy(panel_ref, mine, k, panel_fwd, (turn, k), partner).wait_send()
     for target in range(n_col):

time: 39.3 us -> 38.4 us (0.977)
  Pallas kernels: 36.3 us -> 35.5 us
    pallas_call x1, Pallas kernels: 36.3 us -> 35.5 us  [shards(): pl.pallas_call(functools.partial(kernel, (n_row, n_col, window_count, blo...]
where the time goes in v7:
time: 38.4 us; the launch traced here: 37.9 us
  Pallas kernels  35.5 us (92%)
  local copies, waits for them, and re-layouts  1.67 us (4%)
  between operations  0.64 us (2%)
    pallas_call x1, Pallas kernels, shards(): pl.pallas_call(functools.partial(kernel, (n_row, n_col, window_count, blo...  35.5 us
    unnamed x2, local copies, waits for them, and re-layouts  1.67 us

profile of v7, /device:TPU:1, one launch (start us, length us, event | category | flops | bytes accessed | tf_op | source)
XLA Modules:
  0.0 37.9 jit_solution(17533136880576684441)
XLA Ops:
  0.6 35.5 %shard_map.77 = (f32[4,128,128]{2,1,0:T(8,128)S(1)}, f32[512,512]{1,0:T(8,128)S(1)}) custom-call(s32[8]{0:T(128)} %first_hbm.1, s32[8]{0:T(128)} %slot_hbm.1, f32[128,256]{1,0:T(8,128)} %cov_hbm.1, bf16[4,128,128]{2,1,0:T(8,128)(2,1)} %panel_hbm.1, bf16[6,128,128]{2,1,0:T(8,128)(2,1)} %factor_hbm.1, f32[4,128,128]{2,1,0:T(8,128)} %diag_hbm.1), custom_call_target="tpu_custom_call" | custom-call | tf_op jit(solution)/shard_map/pallas_call | solution.py:421
  36.2 0.7 %copy.10 = f32[4,128,128]{2,1,0:T(8,128)} copy(f32[4,128,128]{2,1,0:T(8,128)S(1)} %get-tuple-element.4) | data formatting | bytes 524288
  36.9 1.0 %copy.11 = f32[512,512]{1,0:T(8,128)} copy(f32[512,512]{1,0:T(8,128)S(1)} %get-tuple-element.5) | data formatting | bytes 2097152
